TPU v7x, 128 devices: a whole 4x4x4 slice. The times are simulated.
128 devices in a mesh: blk: 32 (over x, y, core), mp: 4 (over z).
Axes of the slice: x: 4, y: 4, z: 4, core: 2. Of those that a mesh axis runs over, the one named last changes fastest.
Arguments:
- hidden: bfloat16 [144, 3584], replicated, may hold values from -6 to 6
- medusa_w: bfloat16 [2, 3584, 3584], P(None, 'blk', 'mp'), may hold values from -0.09375 to 0.09375
- embedding: bfloat16 [131072, 3584], P(('blk', 'mp')), may hold values from -0.5 to 0.5
- cand_ids: int32 [2, 144, 10], replicated, may hold values from 0 to 131071
- tree_q: bfloat16 [12, 48, 4096], P(None, None, 'mp'), may hold values from -6 to 6
- tree_key_value: bfloat16 [2, 12, 48, 2048], P(None, None, None, 'mp'), may hold values from -6 to 6
- prompt_key_value: bfloat16 [2, 32, 2048, 2048], P(None, 'blk', None, 'mp'), may hold values from -6 to 6
- block_group: int32 [32], P('blk'), may hold values from 0 to 11, as said below
- block_len: int32 [32], P('blk'), may hold values from 1 to 2048
- block_empty: int32 [32], P('blk'), may hold values 0 or 1
- parents: int32 [12, 48], replicated, may hold values from 0 to 46, as said below
- out_weight: bfloat16 [4096, 3584], P('mp'), may hold values from -0.09375 to 0.09375
- post_gain: float32 [3584], replicated, may hold values from 0.5 to 1.5
- resid: bfloat16 [576, 3584], P('blk'), may hold values from -6 to 6
Outputs:
- draft_logprob: float32 [2, 144, 10], replicated
- layer_out: bfloat16 [576, 3584], P('blk')
Inputs may be any that keep to these rules, and one draw needn't show every extreme that they name: `block_group`: every group number from 0 to min(12, 32) - 1 owns at least one block. `parents`: entry 0 of each row is 0; entry i for i >= 1 is below i; some group's last token has parent 48 - 2.
All inputs are finite; a program needn't handle non-finite values. No bound on the sum of `block_empty` on one device may be relied on, other than what follows from the above.
Results may differ from a plain program's by a relative error of at most 0.005.
Values may be sent and summed in bfloat16 or wider, within the bound.
A program may use at most 128 MiB of HBM per device.

v0:
```python
import jax
import jax.numpy as jnp
from jax import lax
from jax.sharding import PartitionSpec as P

HEAD_SIZE = 256


def capped(values, limit):
    return limit * jnp.tanh(values / limit)


def ancestry(parents):
    count = parents.shape[1]
    column = jnp.arange(count, dtype=jnp.int32)
    linked = (parents[:, :, None] == column[None, None, :]) & (column[None, :, None] > 0)
    reach = jnp.eye(count, dtype=jnp.float32)[None] + linked.astype(jnp.float32)
    for sweep in range(count.bit_length()):
        reach = jnp.minimum(
            jnp.einsum("gij,gjk->gik", reach, reach, precision=lax.Precision.HIGHEST), 1.0
        )
    return reach


def attend(queries, keys, values, mask):
    rows = queries.shape[0]
    length = keys.shape[0]
    kv_heads = keys.shape[1] // HEAD_SIZE
    repeats = queries.shape[1] // keys.shape[1]
    query_view = queries.reshape(rows, kv_heads, repeats, HEAD_SIZE)
    key_view = keys.reshape(length, kv_heads, HEAD_SIZE)
    value_view = values.reshape(length, kv_heads, HEAD_SIZE)
    scores = jnp.einsum(
        "qhrd,khd->hrqk", query_view, key_view, preferred_element_type=jnp.float32
    ) * HEAD_SIZE ** (-0.5)
    weights = jnp.exp(capped(scores, 50.0)) * mask[None, None]
    denominator = jnp.sum(weights, -1).transpose(2, 0, 1).reshape(rows, kv_heads * repeats)
    numerator = jnp.einsum(
        "hrqk,khd->qhrd",
        weights.astype(jnp.bfloat16),
        value_view,
        preferred_element_type=jnp.float32,
    )
    return (numerator.reshape(rows, kv_heads * repeats * HEAD_SIZE), denominator)


def per_device(
    hidden,
    medusa_w,
    embedding,
    cand_ids,
    tree_q,
    tree_key_value,
    prompt_key_value,
    block_group,
    block_len,
    block_empty,
    parents,
    out_weight,
    post_gain,
    resid,
):
    units = medusa_w.shape[2]
    inner = jnp.einsum(
        "rd,mdu->mru",
        hidden,
        lax.all_gather(medusa_w, "blk", axis=1, tiled=True),
        preferred_element_type=jnp.float32,
    )
    own_cols = lax.dynamic_slice_in_dim(hidden, lax.axis_index("mp") * units, units, 1).astype(
        jnp.float32
    )
    fresh = (own_cols[None] + jax.nn.silu(inner)).astype(jnp.bfloat16)
    full_fresh = lax.all_gather(fresh, "mp", axis=2, tiled=True)
    logits = capped(
        jnp.einsum("mrd,vd->mrv", full_fresh, embedding, preferred_element_type=jnp.float32), 30.0
    )
    totals = jnp.sum(jnp.exp(logits), -1)
    vocab_dev = embedding.shape[0]
    first_id = lax.axis_index(("blk", "mp")) * vocab_dev
    local_ids = cand_ids - first_id
    match = local_ids[..., None] == jnp.arange(vocab_dev, dtype=jnp.int32)
    picked = jnp.sum(jnp.where(match, logits[:, :, None, :], 0.0), -1)
    totals, picked = lax.psum((totals, picked), ("blk", "mp"))
    draft_logprob = picked - jnp.log(totals)[..., None]
    groups, tree_size, features = tree_q.shape
    keys = prompt_key_value[0, 0]
    values = prompt_key_value[1, 0]
    length = keys.shape[0]
    group = block_group[0]
    key_ok = ((jnp.arange(length, dtype=jnp.int32) < block_len[0]) & (block_empty[0] == 0)).astype(
        jnp.float32
    )
    row_group = jnp.arange(groups * tree_size, dtype=jnp.int32) // tree_size
    mask = (row_group == group).astype(jnp.float32)[:, None] * key_ok[None, :]
    numer, denom = attend(tree_q.reshape(groups * tree_size, features), keys, values, mask)
    rows_dev = groups * tree_size // lax.axis_size("blk")
    first_row = lax.axis_index("blk") * rows_dev
    summed = lax.psum((numer, denom), "blk")
    numer = lax.dynamic_slice_in_dim(summed[0], first_row, rows_dev, 0)
    denom = lax.dynamic_slice_in_dim(summed[1], first_row, rows_dev, 0)
    reach = ancestry(parents)
    tree_numer, tree_denom = jax.vmap(attend)(tree_q, tree_key_value[0], tree_key_value[1], reach)
    heads_dev = tree_denom.shape[2]
    tree_numer = lax.dynamic_slice_in_dim(
        tree_numer.reshape(groups * tree_size, features), first_row, rows_dev, 0
    )
    tree_denom = lax.dynamic_slice_in_dim(
        tree_denom.reshape(groups * tree_size, heads_dev), first_row, rows_dev, 0
    )
    numer = numer + tree_numer
    denom = denom + tree_denom
    heads_out = (
        (numer.reshape(rows_dev, heads_dev, HEAD_SIZE) / denom[..., None])
        .reshape(rows_dev, features)
        .astype(jnp.bfloat16)
    )
    attn = lax.psum(jnp.dot(heads_out, out_weight, preferred_element_type=jnp.float32), "mp")
    normed = attn * lax.rsqrt(jnp.mean(attn * attn, -1, keepdims=True) + 1e-06) * post_gain
    layer_out = (normed + resid.astype(jnp.float32)).astype(jnp.bfloat16)
    return (draft_logprob, layer_out)


def solution(mesh):
    placed = (
        P(),
        P(None, "blk", "mp"),
        P(("blk", "mp"), None),
        P(),
        P(None, None, "mp"),
        P(None, None, None, "mp"),
        P(None, "blk", None, "mp"),
        P("blk"),
        P("blk"),
        P("blk"),
        P(),
        P("mp", None),
        P(),
        P("blk", None),
    )
    return jax.shard_map(
        per_device, mesh=mesh, in_specs=placed, out_specs=(P(), P("blk", None)), check_vma=False
    )
```

profile of v0, /device:TPU:1, one launch (start us, length us, event | category | flops | bytes accessed | tf_op | source)
XLA Modules:
  0.0 381.7 jit_solution(4261685247920140671)
XLA Ops:
  7.2 0.0 all-reduce.4.cloned.1.call-start
  7.2 4.4 %fusion.51 = (bf16[1,1,2048,512]{3,2,1,0:T(8,128)(2,1)}, bf16[1,1,2048,512]{3,2,1,0:T(8,128)(2,1)}) fusion(bf16[2,1,2048,512]{3,2,1,0:T(8,128)(2,1)} %param.20), kind=kLoop, calls=%fused_computation.70 | loop fusion | bytes 8388608 | tf_op jit(solution)/shard_map/slice | solution.py:88
  11.6 2.9 copy.79
  16.5 3.3 reshape_reshape.3
  19.8 4.0 %copy.80 = bf16[1,1,2048,512]{2,3,1,0:T(8,128)(2,1)} copy(bf16[1,1,2048,512]{3,2,1,0:T(8,128)(2,1)} %get-tuple-element.6) | data formatting | bytes 4194304
  23.8 0.4 broadcast_multiply_fusion
  24.2 10.5 %fusion = (f32[2,2,576]{2,1,0:T(2,128)}, f32[2,2048,576,2]{1,2,3,0:T(8,128)}) fusion(f32[576,2048]{1,0:T(8,128)S(1)} %broadcast_multiply_fusion, bf16[2048,2,256,1]{0,2,3,1:T(8,128)(2,1)S(1)} %bitcast.83, bf16[576,2,2,256]{3,2,1,0:T(2,128)(2,1)S(1)} %reshape_reshape.3), kind=kOutput, calls=%fused_computation.1 | convolution fusion | flops 2434791168 | bytes 26878976 | tf_op jit(solution)/shard_map/qhrd,khd->hrqk/dot_general | solution.py:33
  34.7 9.1 %fusion.6 = f32[576,2,2,256]{3,0,2,1:T(8,128)S(1)} fusion(bf16[2048,2,256,1]{0,2,3,1:T(8,128)(2,1)S(1)} %bitcast.85, f32[2,2048,576,2]{1,2,3,0:T(8,128)} %get-tuple-element.15, f32[576,2048]{1,0:T(8,128)S(1)} %broadcast_multiply_fusion), kind=kOutput, calls=%fused_computation.10 | convolution fusion | flops 2434793472 | bytes 28049408 | tf_op jit(solution)/shard_map/hrqk,khd->qhrd/dot_general | solution.py:38
  43.8 1.8 copy.56
  45.6 2.9 reshape.101
  48.6 0.0 all-gather.3.cloned.1.call-start
  48.6 0.7 all-gather.3.cloned.1.call-update
  49.3 0.2 all-reduce.6.cloned.1.call-start
  49.6 0.3 copy-done
  49.8 0.9 reshape.102
  50.7 0.7 reshape.104
  51.4 0.1 fusion.52
  51.5 0.1 reshape_squeeze.14
  51.7 1.4 convolution_minimum_fusion.5
  53.1 0.4 convolution_minimum_fusion.4
  53.5 0.4 convolution_minimum_fusion.3
  53.9 0.4 convolution_minimum_fusion.2
  54.4 0.4 convolution_minimum_fusion.1
  54.8 0.4 convolution_minimum_fusion
  55.2 0.1 copy.59
  55.3 0.9 fusion.53
  56.2 0.1 reshape.105
  56.3 124.9 %psum.38 = f32[576,4]{0,1:T(4,128)S(1)} all-reduce(f32[576,4]{0,1:T(4,128)S(1)} %reshape.104), channel_id=1, replica_groups=mesh['blk'=32,'mp'=4] {'blk'}, use_global_device_ids=true, to_apply=%region_6.7 | all-reduce | flops 2304 | bytes 18432 | tf_op jit(solution)/shard_map/psum | solution.py:99
  181.2 0.1 dynamic-slice_add_fusion
  181.3 0.1 copy.64
  181.4 0.1 div.48
  181.5 0.1 reshape_squeeze.15
  181.7 0.5 convolution_bitcast_fusion
  182.2 1.8 copy.62
  184.1 2.9 reshape.103
  187.0 0.0 all-reduce.4.cloned.1.call-done
  187.1 5.1 %fusion.39 = f32[18,3584]{1,0:T(8,128)} fusion(bf16[1024,3584]{1,0:T(8,128)(2,1)} %param.25, f32[18,1024]{1,0:T(8,128)S(1)} %bitcast.87, f32[576,1024]{1,0:T(8,128)} %reshape.103, s32[]{:T(128)S(6)} %select_n.25, f32[576,1024]{1,0:T(8,128)} %all-reduce.4.cloned.1.call-done), kind=kOutput, calls=%fused_computation.47 | convolution fusion | flops 132175872 | bytes 7868420 | tf_op jit(solution)/shard_map/dot_general | solution.py:118
  192.2 0.3 all-gather.5.cloned.1.call-start
  192.4 32.7 %all-gather.3.cloned.1.call-done = bf16[2,3584,896]{2,1,0:T(8,128)(2,1)} async-done(((bf16[2,112,896]{2,1,0:T(8,128)(2,1)}), bf16[2,3584,896]{2,1,0:T(8,128)(2,1)}) %all-gather.3.cloned.1.call-update) | async-done | bytes 12845072 | tf_op jit(solution)/shard_map/all_gather | solution.py:67
  225.2 7.6 %add_convert_fusion = bf16[2,144,896]{2,1,0:T(8,128)(2,1)} fusion(bf16[2,3584,896]{2,1,0:T(8,128)(2,1)} %all-gather.3.cloned.1.call-done, bf16[144,3584]{1,0:T(8,128)(2,1)S(1)} %copy-done.4, f32[144,896]{1,0:T(8,128)S(1)} %dynamic-slice_convert_fusion), kind=kOutput, calls=%fused_computation.32 | convolution fusion | flops 1851236352 | bytes 14909440 | tf_op jit(solution)/shard_map/rd,mdu->mru/dot_general | solution.py:64
  232.8 34.1 %all-reduce.6.cloned.1.call-done = f32[18,3584]{1,0:T(8,128)} async-done(((f32[18,3584]{1,0:T(8,128)}), f32[18,3584]{1,0:T(8,128)}) %all-reduce.6.cloned.1.call-update) | async-done | bytes 258064 | tf_op jit(solution)/shard_map/psum | solution.py:118
  266.9 1.1 multiply_reduce_fusion
  268.0 1.8 add_convert_fusion.1
  269.8 31.7 %all-gather.5.cloned.1.call-done = bf16[2,144,3584]{2,1,0:T(8,128)(2,1)} async-done(((bf16[2,144,896]{2,1,0:T(8,128)(2,1)}), bf16[2,144,3584]{2,1,0:T(8,128)(2,1)}) %all-gather.5.cloned.1.call-update) | async-done | bytes 2064400 | tf_op jit(solution)/shard_map/all_gather | solution.py:74
  301.5 6.2 %exponential_reduce_fusion = (f32[2,144]{1,0:T(2,128)S(1)}, f32[2,144,1024]{2,1,0:T(8,128)S(1)}) fusion(bf16[2,144,3584]{2,1,0:T(8,128)(2,1)} %all-gather.5.cloned.1.call-done, bf16[1024,3584]{1,0:T(8,128)(2,1)} %param.16), kind=kOutput, calls=%fused_computation.24 | convolution fusion | flops 2114813696 | bytes 10585216 | tf_op jit(solution)/shard_map/mrd,vd->mrv/dot_general | solution.py:76
  307.8 1.8 select_reduce_fusion
  309.6 64.9 %all-reduce = (f32[2,144,10]{1,2,0:T(8,128)S(1)}, f32[2,144]{1,0:T(2,128)S(1)}) all-reduce(f32[2,144,10]{1,2,0:T(8,128)S(1)} %select_reduce_fusion, f32[2,144]{1,0:T(2,128)S(1)} %get-tuple-element.10), channel_id=1, replica_groups=mesh['blk'=32,'mp'=4] {'blk','mp'}, use_global_device_ids=true, to_apply=%region_1.2 | all-reduce | flops 3168 | bytes 25344 | tf_op jit(solution)/shard_map/psum | solution.py:84
  374.5 0.6 copy.65
  (29 shorter events, 0.2 us)
Async XLA Ops:
  7.2 179.9 %all-reduce.4.cloned.1.call-start = ((), (), s32[]{:S(2)}) async-start(), calls=%async_computation.2 | async-start | bytes 4718592 | tf_op jit(solution)/shard_map/psum | solution.py:99
  24.2 10.5 %copy-start.1 = (bf16[1,1,2048,512]{2,3,1,0:T(8,128)(2,1)S(1)}, bf16[1,1,2048,512]{2,3,1,0:T(8,128)(2,1)}, u32[]{:S(2)}) copy-start(bf16[1,1,2048,512]{2,3,1,0:T(8,128)(2,1)} %copy.80) | copy-start | bytes 6291460
  48.6 1.3 copy-start
  48.6 2.9 copy-start.2
  48.6 176.6 %all-gather.3.cloned.1.call-start = ((), (), s32[]{:S(2)}) async-start(), calls=%async_computation | async-start | bytes 13246464 | tf_op jit(solution)/shard_map/all_gather | solution.py:67
  49.3 217.6 %all-reduce.6.cloned.1.call-start = ((), (), s32[]{:S(2)}) async-start(), calls=%async_computation.3 | async-start | bytes 688128 | tf_op jit(solution)/shard_map/psum | solution.py:118
  184.0 3.0 copy-start.4
  192.1 40.7 %copy-start.5 = (s32[2,144,10]{1,0,2:T(2,128)S(1)}, s32[2,144,10]{1,0,2:T(2,128)}, u32[]{:S(2)}) copy-start(s32[2,144,10]{1,0,2:T(2,128)} %param.17) | copy-start | bytes 34564
  192.2 75.9 %copy-start.3 = (bf16[18,3584]{1,0:T(8,128)(2,1)S(1)}, bf16[18,3584]{1,0:T(8,128)(2,1)}, u32[]{:S(2)}) copy-start(bf16[18,3584]{1,0:T(8,128)(2,1)} %param.27) | copy-start | bytes 387076
  192.2 75.9 %copy-start.6 = (f32[3584]{0:T(1024)S(1)}, f32[3584]{0:T(1024)}, u32[]{:S(2)}) copy-start(f32[3584]{0:T(1024)} %param.26) | copy-start | bytes 43012
  192.2 109.4 %all-gather.5.cloned.1.call-start = ((), (), s32[]{:S(2)}) async-start(), calls=%async_computation.1 | async-start | bytes 2580480 | tf_op jit(solution)/shard_map/all_gather | solution.py:74
Sparse Core Ops, SparseCore 0:
  48.7 110.4 all-reduce.3
  161.6 63.5 all-gather.2
  227.5 39.3 all-reduce.5
  268.4 33.0 all-gather.4
where the time goes:
time: 382 us
  blocking collectives  190 us (50%)
  waiting for transfers between devices  99.3 us (26%)
  matrix products  43.3 us (11%)
  local copies, waits for them, and re-layouts  27.5 us (7%)
  between operations  16 us (4%)
  other arithmetic  5.25 us (1%)
    psum x1, blocking collectives, per_device(): summed = lax.psum((numer, denom), 'blk')  125 us
    psum x1, blocking collectives, per_device(): totals, picked = lax.psum((totals, picked), ('blk', 'mp'))  64.9 us
    psum x1, waiting for transfers between devices, per_device(): lax.psum(jnp.dot(heads_out, out_weight, preferred_element_type=jnp.float3...  34.1 us
    all_gather x1, waiting for transfers between devices, per_device(): lax.all_gather(medusa_w, 'blk', axis=1, tiled=True)  32.7 us
    all_gather x1, waiting for transfers between devices, per_device(): full_fresh = lax.all_gather(fresh, 'mp', axis=2, tiled=True)  31.7 us
    dot_general x2, matrix products, attend(): jnp.einsum('qhrd,khd->hrqk', query_view, key_view, preferred_element_type...  11.3 us
    dot_general x2, matrix products, attend(): jnp.einsum('hrqk,khd->qhrd', weights.astype(jnp.bfloat16), value_view, pr...  9.63 us
    unnamed x19, local copies, waits for them, and re-layouts  7.84 us
  transfers between devices with their start and end apart: 4, of which 3 were waited for; matrix products, arithmetic and copies ran while one was open for 7% of the time, Pallas kernels for 0%

commit v1 on v0

--- a/solution.py
+++ b/solution.py
@@ -2,6 +2,7 @@
 import jax.numpy as jnp
 from jax import lax
 from jax.sharding import PartitionSpec as P
+from jax.lax import all_gather
 
 HEAD_SIZE = 256
 
@@ -60,6 +61,11 @@
     post_gain,
     resid,
 ):
+
+    def attach_windows(xin):
+        local_out = jnp.sum(all_gather(xin, "mp"), 0)
+        return local_out
+
     units = medusa_w.shape[2]
     inner = jnp.einsum(
         "rd,mdu->mru",
@@ -115,7 +121,7 @@
         .reshape(rows_dev, features)
         .astype(jnp.bfloat16)
     )
-    attn = lax.psum(jnp.dot(heads_out, out_weight, preferred_element_type=jnp.float32), "mp")
+    attn = attach_windows(jnp.dot(heads_out, out_weight, preferred_element_type=jnp.float32))
     normed = attn * lax.rsqrt(jnp.mean(attn * attn, -1, keepdims=True) + 1e-06) * post_gain
     layer_out = (normed + resid.astype(jnp.float32)).astype(jnp.bfloat16)
     return (draft_logprob, layer_out)

time: 382 us -> 322 us (0.84)
  waiting for transfers between devices: 99.3 us -> 24.6 us
  blocking collectives: 190 us -> 205 us
    psum x1 -> x0, waiting for transfers between devices: 34.1 us -> none  [per_device(): lax.psum(jnp.dot(heads_out, out_weight, preferred_element_type=jnp.float3...]
    all_gather x1, waiting for transfers between devices: 31.7 us -> 0.01 us  [per_device(): full_fresh = lax.all_gather(fresh, 'mp', axis=2, tiled=True)]
    all_gather x0 -> x1, blocking collectives: none -> 14 us  [attach_windows(): local_out = jnp.sum(all_gather(xin, 'mp'), 0)]
    all_gather x1, waiting for transfers between devices: 32.7 us -> 23.9 us  [per_device(): lax.all_gather(medusa_w, 'blk', axis=1, tiled=True)]
    psum x1, blocking collectives: 64.9 us -> 70.1 us  [per_device(): totals, picked = lax.psum((totals, picked), ('blk', 'mp'))]
  transfers between devices with their start and end apart: 4 -> 3, of which waited for: 3 -> 1; matrix products, arithmetic and copies ran while one was open for 7% -> 20% of each run, Pallas kernels for 0% -> 0%
where the time goes in v1:
time: 322 us
  blocking collectives  205 us (64%)
  matrix products  42.9 us (13%)
  local copies, waits for them, and re-layouts  28.4 us (9%)
  waiting for transfers between devices  24.6 us (8%)
  between operations  16 us (5%)
  other arithmetic  4.36 us (1%)
    psum x1, blocking collectives, per_device(): summed = lax.psum((numer, denom), 'blk')  121 us
    psum x1, blocking collectives, per_device(): totals, picked = lax.psum((totals, picked), ('blk', 'mp'))  70.1 us
    all_gather x1, waiting for transfers between devices, per_device(): lax.all_gather(medusa_w, 'blk', axis=1, tiled=True)  23.9 us
    all_gather x1, blocking collectives, attach_windows(): local_out = jnp.sum(all_gather(xin, 'mp'), 0)  14 us
    dot_general x2, matrix products, attend(): jnp.einsum('qhrd,khd->hrqk', query_view, key_view, preferred_element_type...  12.1 us
    dot_general x2, matrix products, attend(): jnp.einsum('hrqk,khd->qhrd', weights.astype(jnp.bfloat16), value_view, pr...  9.64 us
    unnamed x19, local copies, waits for them, and re-layouts  8.62 us
    dot_general x1, matrix products, per_device(): jnp.einsum('rd,mdu->mru', hidden, lax.all_gather(medusa_w, 'blk', axis=1,...  7.92 us
  transfers between devices with their start and end apart: 3, of which 1 were waited for; matrix products, arithmetic and copies ran while one was open for 20% of the time, Pallas kernels for 0%

profile of v1, /device:TPU:1, one launch (start us, length us, event | category | flops | bytes accessed | tf_op | source)
XLA Modules:
  0.0 321.9 jit_solution(3027131254926797666)
XLA Ops:
  7.2 0.0 all-gather.5.cloned.1.call-start
  7.2 0.7 all-gather.5.cloned.1.call-update
  7.9 0.0 all-reduce.3.cloned.1.call-start
  7.9 4.4 %fusion.50 = (bf16[1,1,2048,512]{3,2,1,0:T(8,128)(2,1)}, bf16[1,1,2048,512]{3,2,1,0:T(8,128)(2,1)}) fusion(bf16[2,1,2048,512]{3,2,1,0:T(8,128)(2,1)} %param.20), kind=kLoop, calls=%fused_computation.70 | loop fusion | bytes 8388608 | tf_op jit(solution)/shard_map/slice | solution.py:94
  12.4 2.9 copy.79
  17.2 3.3 %reshape_reshape.3 = bf16[576,2,2,256]{3,2,1,0:T(2,128)(2,1)S(1)} reshape(bf16[12,48,1024]{2,1,0:T(8,128)(2,1)} %param.18) | data formatting | bytes 2359296 | tf_op jit(solution)/shard_map/reshape;reshape | solution.py:31
  20.6 4.0 %copy.80 = bf16[1,1,2048,512]{2,3,1,0:T(8,128)(2,1)} copy(bf16[1,1,2048,512]{3,2,1,0:T(8,128)(2,1)} %get-tuple-element.6) | data formatting | bytes 4194304
  24.6 0.4 broadcast_multiply_fusion
  25.0 9.9 %fusion = (f32[2,2,576]{2,1,0:T(2,128)S(1)}, f32[2,2048,576,2]{1,2,3,0:T(8,128)}) fusion(f32[576,2048]{1,0:T(8,128)S(1)} %broadcast_multiply_fusion, bf16[2048,2,256,1]{0,2,3,1:T(8,128)(2,1)S(1)} %bitcast.85, bf16[576,2,2,256]{3,2,1,0:T(2,128)(2,1)S(1)} %reshape_reshape.3), kind=kOutput, calls=%fused_computation.1 | convolution fusion | flops 2434791168 | bytes 26878976 | tf_op jit(solution)/shard_map/qhrd,khd->hrqk/dot_general | solution.py:34
  34.9 9.1 %fusion.6 = f32[576,2,2,256]{3,0,2,1:T(8,128)S(1)} fusion(bf16[2048,2,256,1]{0,2,3,1:T(8,128)(2,1)S(1)} %bitcast.87, f32[2,2048,576,2]{1,2,3,0:T(8,128)} %get-tuple-element.15, f32[576,2048]{1,0:T(8,128)S(1)} %broadcast_multiply_fusion), kind=kOutput, calls=%fused_computation.11 | convolution fusion | flops 2434793472 | bytes 28049408 | tf_op jit(solution)/shard_map/hrqk,khd->qhrd/dot_general | solution.py:39
  44.0 1.8 copy.56
  45.8 2.9 reshape.101
  48.7 0.0 all-reduce.3.cloned.1.call-update
  48.8 0.2 all-gather.7.cloned.1.call-start
  49.0 1.0 copy-done.2
  50.0 0.1 fusion.51
  50.1 0.6 convolution_minimum_fusion.5
  50.7 0.4 convolution_minimum_fusion.4
  51.1 0.4 convolution_minimum_fusion.3
  51.6 0.4 convolution_minimum_fusion.2
  52.0 1.0 dynamic-slice_convert_fusion
  53.0 0.4 convolution_minimum_fusion.1
  53.4 23.9 %all-gather.5.cloned.1.call-done = bf16[2,3584,896]{2,1,0:T(8,128)(2,1)} async-done(((bf16[2,112,896]{2,1,0:T(8,128)(2,1)}), bf16[2,3584,896]{2,1,0:T(8,128)(2,1)}) %all-gather.5.cloned.1.call-update) | async-done | bytes 12845072 | tf_op jit(solution)/shard_map/all_gather | solution.py:73
  77.3 7.9 %add_convert_fusion = bf16[2,144,896]{2,1,0:T(8,128)(2,1)} fusion(bf16[2,3584,896]{2,1,0:T(8,128)(2,1)} %all-gather.5.cloned.1.call-done, bf16[144,3584]{1,0:T(8,128)(2,1)} %param.14, f32[144,896]{1,0:T(8,128)S(1)} %dynamic-slice_convert_fusion), kind=kOutput, calls=%fused_computation.33 | convolution fusion | flops 1851236352 | bytes 14909440 | tf_op jit(solution)/shard_map/rd,mdu->mru/dot_general | solution.py:70
  85.2 0.4 convolution_minimum_fusion
  85.7 1.7 reshape.102
  87.4 0.1 reshape_squeeze.14
  87.5 0.1 copy.59
  87.7 2.2 fusion.52
  89.9 0.1 reshape.105
  90.0 121.3 %psum.31 = f32[576,4]{0,1:T(4,128)S(1)} all-reduce(f32[576,4]{0,1:T(4,128)S(1)} %reshape.104), channel_id=1, replica_groups=mesh['blk'=32,'mp'=4] {'blk'}, use_global_device_ids=true, to_apply=%region_6.7 | all-reduce | flops 2304 | bytes 18432 | tf_op jit(solution)/shard_map/psum | solution.py:105
  211.3 0.1 dynamic-slice_add_fusion
  211.4 0.1 copy.64
  211.5 0.1 div.48
  211.7 0.1 reshape_squeeze.15
  211.8 0.5 convolution_bitcast_fusion.1
  212.3 1.8 copy.62
  214.2 2.9 reshape.103
  217.1 0.0 all-reduce.3.cloned.1.call-done
  217.2 4.3 %convolution_bitcast_fusion = f32[1,18,3584]{2,1,0:T(8,128)S(1)} fusion(bf16[1024,3584]{1,0:T(8,128)(2,1)} %param.25, f32[18,1024]{1,0:T(8,128)S(1)} %bitcast.89, f32[576,1024]{1,0:T(8,128)} %reshape.103, s32[]{:T(128)S(6)} %select_n.25, f32[576,1024]{1,0:T(8,128)} %all-reduce.3.cloned.1.call-done), kind=kOutput, calls=%fused_computation.8 | convolution fusion | flops 132175872 | bytes 7868420 | tf_op jit(solution)/shard_map/dot_general | solution.py:124
  221.5 14.0 %all-gather.1 = f32[4,18,3584]{2,1,0:T(8,128)S(1)} all-gather(f32[1,18,3584]{2,1,0:T(8,128)S(1)} %convolution_bitcast_fusion), channel_id=2, replica_groups=mesh['blk'=32,'mp'=4] {'mp'}, dimensions={0}, use_global_device_ids=true | all-gather | bytes 1290240 | tf_op jit(solution)/shard_map/all_gather | solution.py:66
  235.5 0.1 reduce_sum.58
  235.6 0.1 multiply_reduce_fusion
  235.8 0.8 add_convert_fusion.1
  236.6 6.2 %exponential_reduce_fusion = (f32[2,144]{1,0:T(2,128)S(1)}, f32[2,144,1024]{2,1,0:T(8,128)S(1)}) fusion(bf16[2,144,3584]{2,1,0:T(8,128)(2,1)} %all-gather.7.cloned.1.call-done, bf16[1024,3584]{1,0:T(8,128)(2,1)} %param.16), kind=kOutput, calls=%fused_computation.25 | convolution fusion | flops 2114813696 | bytes 10585216 | tf_op jit(solution)/shard_map/mrd,vd->mrv/dot_general | solution.py:82
  242.8 1.8 select_reduce_fusion
  244.6 70.1 %all-reduce = (f32[2,144,10]{1,2,0:T(8,128)S(1)}, f32[2,144]{1,0:T(2,128)S(1)}) all-reduce(f32[2,144,10]{1,2,0:T(8,128)S(1)} %select_reduce_fusion, f32[2,144]{1,0:T(2,128)S(1)} %get-tuple-element.10), channel_id=1, replica_groups=mesh['blk'=32,'mp'=4] {'blk','mp'}, use_global_device_ids=true, to_apply=%region_1.2 | all-reduce | flops 3168 | bytes 25344 | tf_op jit(solution)/shard_map/psum | solution.py:90
  314.7 0.6 copy.65
  (28 shorter events, 0.2 us)
Async XLA Ops:
  7.2 70.1 %all-gather.5.cloned.1.call-start = ((), (), s32[]{:S(2)}) async-start(), calls=%async_computation | async-start | bytes 13246464 | tf_op jit(solution)/shard_map/all_gather | solution.py:73
  7.9 209.3 %all-reduce.3.cloned.1.call-start = ((), (), s32[]{:S(2)}) async-start(), calls=%async_computation.2 | async-start | bytes 4718592 | tf_op jit(solution)/shard_map/psum | solution.py:105
  25.0 9.9 %copy-start.1 = (bf16[1,1,2048,512]{2,3,1,0:T(8,128)(2,1)S(1)}, bf16[1,1,2048,512]{2,3,1,0:T(8,128)(2,1)}, u32[]{:S(2)}) copy-start(bf16[1,1,2048,512]{2,3,1,0:T(8,128)(2,1)} %copy.80) | copy-start | bytes 6291460
  48.7 1.3 copy-start.2
  48.7 1.4 copy-start.6
  48.8 187.8 %all-gather.7.cloned.1.call-start = ((), (), s32[]{:S(2)}) async-start(), calls=%async_computation.1 | async-start | bytes 2580480 | tf_op jit(solution)/shard_map/all_gather | solution.py:80
  53.4 32.2 %copy-start = (bf16[12,48,1024]{2,1,0:T(8,128)(2,1)S(1)}, bf16[12,48,1024]{2,1,0:T(8,128)(2,1)}, u32[]{:S(2)}) copy-start(bf16[12,48,1024]{2,1,0:T(8,128)(2,1)} %param.18) | copy-start | bytes 3538948
  214.1 3.0 copy-start.4
  221.5 14.3 %copy-start.3 = (bf16[18,3584]{1,0:T(8,128)(2,1)S(1)}, bf16[18,3584]{1,0:T(8,128)(2,1)}, u32[]{:S(2)}) copy-start(bf16[18,3584]{1,0:T(8,128)(2,1)} %param.27) | copy-start | bytes 387076
  221.5 14.3 %copy-start.5 = (f32[3584]{0:T(1024)S(1)}, f32[3584]{0:T(1024)}, u32[]{:S(2)}) copy-start(f32[3584]{0:T(1024)} %param.26) | copy-start | bytes 43012
Sparse Core Ops, SparseCore 0:
  10.4 66.8 all-gather.4
  80.6 106.3 all-reduce.2
  188.7 30.6 all-gather.6
